TPU v7x, 256 devices: a whole 4x4x8 slice. The times are simulated.
256 devices in a mesh: ctx: 16 (over z, core), exp: 16 (over x, y).
Axes of the slice: x: 4, y: 4, z: 8, core: 2. Of those that a mesh axis runs over, the one named last changes fastest.
Arguments:
- inner_input: bfloat16 [8192, 8192], P('ctx', 'exp'), may hold values from -6 to 6
- gate_input: bfloat16 [8192, 8192], P('ctx', 'exp'), may hold values from -6 to 6
- coupling_input: bfloat16 [8192, 256], P('ctx'), may hold values from -6 to 6
- step_input: float32 [8192, 128], P('ctx', 'exp'), may hold values from -7 to 140
- conv_inner: float32 [4, 8192], P(None, 'exp'), may hold values from -3 to 3
- conv_coupling: float32 [4, 256], replicated, may hold values from -3 to 3
- decay_log: float32 [128], P('exp'), may hold values from -5.3 to -2.5
- skip_gain: float32 [128], P('exp'), may hold values from 0.5 to 2
- norm_gain: float32 [8192], P('exp'), may hold values from 0.1 to 1.9
- out_weight: bfloat16 [8192, 4096], P('exp'), may hold values from -0.0625 to 0.0625
- residual: bfloat16 [8192, 4096], P(('ctx', 'exp')), may hold values from -6 to 6
- moe_gain: float32 [4096], replicated, may hold values from 0.1 to 1.9
- router_weight: bfloat16 [4096, 72], replicated, may hold values from -0.1875 to 0.1875
- routes: int32 [8192, 10], P(('ctx', 'exp')), may hold values from 0 to 71, all different within a row
- priority: int32 [256, 32], P(('ctx', 'exp')), may hold values from 0 to 31, each once within a row
- expert_in: bfloat16 [16, 4096, 1536], P('exp', 'ctx'), may hold values from -0.09375 to 0.09375
- expert_out: bfloat16 [16, 4096, 768], P('exp', 'ctx'), may hold values from -0.21875 to 0.21875
Outputs:
- hidden: float32 [8192, 4096], P(('ctx', 'exp'))
- moe_out: float32 [8192, 4096], P(('ctx', 'exp'))
Inputs may be any that keep to these rules, and one draw needn't show every extreme that they name: `routes`: each token names 10 different experts. `priority`: the 32 tokens of each row carry distinct priorities.
All inputs are finite; a program needn't handle non-finite values.
Results may differ from a plain program's by a relative error of at most 0.029.
Values may be sent and summed in bfloat16 or wider, within the bound.
A program may use at most 128 MiB of HBM per device.

v0:
```python
import jax
import jax.numpy as jnp
from jax import lax
from jax.sharding import PartitionSpec as P

HDIM = 64
STATE = 128
KCONV = 4
NEXP = 72
TOPK = 10
FFE = 768
SPAN = 256
INNER = 8192
EPS = 1e-05
HIGH = lax.Precision.HIGHEST


def shifted(array, axis, by):
    devices = lax.axis_size(axis)
    pairs = [(i, i + by) for i in range(devices) if 0 <= i + by < devices]
    return lax.ppermute(array, axis, pairs)


def carried_in(part, axis, combine, identity):
    place = lax.axis_index(axis)
    gathered = jax.tree.map(lambda a: lax.all_gather(a, axis), part)
    state = jax.tree.map(lambda a, e: jnp.zeros_like(a) + jnp.asarray(e, a.dtype), part, identity)

    def one(step, state):
        return combine(
            state, jax.tree.map(lambda a: lax.dynamic_index_in_dim(a, step, 0, False), gathered)
        )

    return lax.fori_loop(0, place, one, state)


def causal_conv(values, before, weight):
    count = values.shape[0]
    padded = jnp.concatenate([before.astype(jnp.float32), values.astype(jnp.float32)], axis=0)
    total = jnp.zeros((count, values.shape[1]), jnp.float32)
    for k in range(KCONV):
        total = total + weight[k][None, :] * padded[k : k + count]
    return jax.nn.silu(total).astype(jnp.bfloat16)


def join_states(earlier, later):
    return (earlier[0] * later[0], later[0][:, None, None] * earlier[1] + later[1])


def body(
    inner_input,
    gate_input,
    coupling_input,
    step_input,
    conv_inner,
    conv_coupling,
    decay_log,
    skip_gain,
    norm_gain,
    out_weight,
    residual,
    moe_gain,
    router_weight,
    routes,
    priority,
    expert_in,
    expert_out,
):
    width = inner_input.shape[1]
    heads = decay_log.shape[0]
    count = inner_input.shape[0]
    blocks = count // SPAN
    edges = jnp.concatenate(
        [inner_input[count - (KCONV - 1) :], coupling_input[count - (KCONV - 1) :]], axis=1
    )
    before = shifted(edges, "ctx", 1)
    inner = causal_conv(inner_input, before[:, :width], conv_inner)
    coupling = causal_conv(coupling_input, before[:, width:], conv_coupling)
    steps = jax.nn.softplus(step_input).reshape(blocks, SPAN, heads)
    inner_parts = inner.reshape(blocks, SPAN, heads, HDIM)
    input_parts = coupling[:, :STATE].reshape(blocks, SPAN, STATE)
    output_parts = coupling[:, STATE:].reshape(blocks, SPAN, STATE)
    rate = steps * (-jnp.exp(decay_log))[None, None, :]
    cums = jnp.cumsum(rate, axis=1)
    scores = jnp.einsum(
        "cin,cjn->cij", output_parts, input_parts, preferred_element_type=jnp.float32
    )
    above = (jnp.arange(SPAN)[:, None] >= jnp.arange(SPAN)[None, :])[None, None]
    flipped = jnp.swapaxes(cums, 1, 2)
    spread = flipped[:, :, :, None] - flipped[:, :, None, :]
    decay = jnp.where(above, jnp.exp(jnp.where(above, spread, 0.0)), 0.0)
    mixing = (scores[:, None] * decay * jnp.swapaxes(steps, 1, 2)[:, :, None, :]).astype(
        jnp.bfloat16
    )
    local = jnp.einsum("chij,cjhp->cihp", mixing, inner_parts, preferred_element_type=jnp.float32)
    inner_wide = inner_parts.astype(jnp.float32)
    tail = jnp.exp(cums[:, -1:, :] - cums) * steps
    states = jnp.einsum(
        "cjh,cjn,cjhp->chnp", tail, input_parts.astype(jnp.float32), inner_wide, precision=HIGH
    )
    drops = jnp.exp(cums[:, -1, :])
    running = jnp.zeros((heads, STATE, HDIM), jnp.float32)
    reach = jnp.ones((heads,), jnp.float32)
    starts = []
    reaches = []
    for k in range(blocks):
        starts.append(running)
        reaches.append(reach)
        running = drops[k][:, None, None] * running + states[k]
        reach = reach * drops[k]
    neutral = (jnp.ones((heads,), jnp.float32), jnp.zeros((heads, STATE, HDIM), jnp.float32))
    incoming = carried_in((reach, running), "ctx", join_states, neutral)[1]
    entry = jnp.stack([reaches[k][:, None, None] * incoming + starts[k] for k in range(blocks)])
    carried = jnp.einsum(
        "cin,cih,chnp->cihp", output_parts.astype(jnp.float32), jnp.exp(cums), entry, precision=HIGH
    )
    mixed = (local + carried + skip_gain[None, None, :, None] * inner_wide).reshape(count, width)
    gated = mixed * jax.nn.silu(gate_input.astype(jnp.float32))
    squares = jnp.sum(gated * gated, axis=1)
    scaled = (gated * norm_gain[None, :]).astype(jnp.bfloat16)
    projected = jnp.dot(scaled, out_weight, preferred_element_type=jnp.float32)
    owned = lax.psum_scatter(
        projected.astype(jnp.bfloat16), "exp", scatter_dimension=0, tiled=True
    ).astype(jnp.float32)
    owned_squares = lax.psum_scatter(squares, "exp", scatter_dimension=0, tiled=True)
    mamba_out = owned * lax.rsqrt(owned_squares / INNER + EPS)[:, None]
    hidden = residual.astype(jnp.float32) + mamba_out
    tokens = hidden.shape[0]
    flight = lax.axis_size("exp")
    capacity = max(2, 2 * tokens * TOPK // NEXP)
    normed = (
        hidden * lax.rsqrt(jnp.mean(hidden * hidden, axis=1) + EPS)[:, None] * moe_gain[None, :]
    ).astype(jnp.bfloat16)
    logits = jnp.dot(normed, router_weight, preferred_element_type=jnp.float32)
    table = routes[:, :, None] == jnp.arange(NEXP, dtype=jnp.int32)[None, None, :]
    picked = jnp.sum(jnp.where(table, logits[:, None, :], 0.0), axis=2)
    raised = jnp.exp(picked)
    probs = raised / jnp.sum(raised, axis=1, keepdims=True)
    match = routes[:, :, None] == jnp.arange(flight, dtype=jnp.int32)[None, None, :]
    member = jnp.sum(match.astype(jnp.int32), axis=1)
    share = jnp.sum(jnp.where(match, probs[:, :, None], 0.0), axis=1).astype(jnp.bfloat16)
    order = priority[0]
    earlier = (order[None, :] < order[:, None]).astype(jnp.int32)
    rank = jnp.sum(earlier[:, :, None] * member[None, :, :], axis=1)
    kept = (member > 0) & (rank < capacity)
    slots = kept[:, :, None] & (
        rank[:, :, None] == jnp.arange(capacity, dtype=jnp.int32)[None, None, :]
    )
    select = jnp.transpose(slots, (1, 2, 0)).astype(jnp.bfloat16)
    outbound = jnp.einsum("fst,td->fsd", select, normed, preferred_element_type=jnp.float32).astype(
        jnp.bfloat16
    )
    arrived = lax.all_to_all(outbound, "exp", split_axis=0, concat_axis=0, tiled=True)
    rows = arrived.reshape(flight * capacity, normed.shape[1])
    slices = lax.axis_size("ctx")
    whole_in = lax.all_gather(expert_in[0], "ctx", axis=0, tiled=True)
    slice_width = rows.shape[1] // slices
    parts = jnp.einsum(
        "rkw,kwf->krf",
        rows.reshape(rows.shape[0], slices, slice_width),
        whole_in.reshape(slices, slice_width, 2 * FFE),
        preferred_element_type=jnp.float32,
    ).astype(jnp.bfloat16)
    units = jnp.sum(lax.optimization_barrier(parts).astype(jnp.float32), axis=0)
    activated = (jax.nn.silu(units[:, :FFE]) * units[:, FFE:]).astype(jnp.bfloat16)
    answer = jnp.einsum(
        "rf,df->rd",
        activated,
        lax.all_gather(expert_out[0], "ctx", axis=0, tiled=True),
        preferred_element_type=jnp.float32,
    ).astype(jnp.bfloat16)
    returned = lax.all_to_all(
        answer.reshape(flight, capacity, answer.shape[1]),
        "exp",
        split_axis=0,
        concat_axis=0,
        tiled=True,
    )
    weights = select * jnp.transpose(share)[:, None, :]
    moe_out = jnp.einsum("fst,fsd->td", weights, returned, preferred_element_type=jnp.float32)
    return (hidden, moe_out)


def solution(mesh):
    placed = (
        P("ctx", "exp"),
        P("ctx", "exp"),
        P("ctx", None),
        P("ctx", "exp"),
        P(None, "exp"),
        P(),
        P("exp"),
        P("exp"),
        P("exp"),
        P("exp", None),
        P(("ctx", "exp"), None),
        P(),
        P(),
        P(("ctx", "exp"), None),
        P(("ctx", "exp"), None),
        P("exp", "ctx", None),
        P("exp", "ctx", None),
    )
    return jax.shard_map(
        body,
        mesh=mesh,
        in_specs=placed,
        out_specs=(P(("ctx", "exp"), None), P(("ctx", "exp"), None)),
        check_vma=False,
    )
```

profile of v0, /device:TPU:32, one launch (start us, length us, event | category | flops | bytes accessed | tf_op | source)
XLA Modules:
  0.0 354.1 jit_solution(14720117451480724429)
XLA Ops:
  7.2 0.8 slice.91
  8.0 0.7 slice.92
  8.7 0.8 copy.91
  9.5 1.9 collective-permute-start
  11.4 0.7 compare_select_fusion
  12.2 0.7 exponential_negate_fusion
  12.9 1.1 reduce-window.6
  14.3 0.7 fusion.63
  15.2 0.8 fusion.66
  16.0 0.9 fusion.65
  16.9 0.6 slice_bitcast_fusion.1
  17.5 1.0 convert_element_type.80
  18.5 1.3 copy.92
  20.4 1.5 multiply_convert_fusion.9
  22.0 0.7 convolution_bitcast_fusion.1
  22.7 0.8 slice_add_fusion
  23.8 19.0 %all-gather.2 = f32[16,1,8]{2,1,0:T(1,128)} all-gather(f32[1,1,8]{2,1,0:T(1,128)S(1)} %get-tuple-element.98), channel_id=1, replica_groups=mesh['ctx'=16,'exp'=16] {'ctx'}, dimensions={0}, use_global_device_ids=true | all-gather | bytes 544 | tf_op jit(solution)/shard_map/all_gather | solution.py:26
  42.9 0.7 add_bitcast_fusion.1
  43.5 1.0 fusion.67
  44.6 24.1 %all-gather.7.cloned.1.call-done = f32[16,8,128,64]{2,3,1,0:T(8,128)} async-done(((f32[1,8,128,64]{2,3,1,0:T(8,128)}), f32[16,8,128,64]{2,3,1,0:T(8,128)}) %all-gather.7.cloned.1.call-update) | async-done | bytes 4194320 | tf_op jit(solution)/shard_map/all_gather | solution.py:26
  68.7 4.1 %while.12 = (s32[]{:T(128)}, f32[8,128,64]{2,1,0:T(8,128)S(1)}, s32[]{:T(128)}, f32[16,8]{1,0:T(8,128)}, f32[16,8,128,64]{2,3,1,0:T(8,128)}, /*index=5*/s32[]{:T(128)}, s32[]{:T(128)}, s32[]{:T(128)}) while((s32[]{:T(128)}, f32[8,128,64]{2,1,0:T(8,128)S(1)}, s32[]{:T(128)}, f32[16,8]{1,0:T(8,128)}, f32[16,8,128,64]{2,3,1,0:T(8,128)}, ...), condition=%wide.region_3.4_spmd, body=%wide.region_2.3_spmd.sunk | while | flops 131077 | bytes 1835231 | solution.py:34
  68.8 1.0 constant_dynamic-slice_fusion.2
  69.9 0.7 dynamic-slice_bitcast_fusion.2
  70.8 1.0 constant_dynamic-slice_fusion.2
  72.0 0.7 dynamic-slice_bitcast_fusion.2
  73.0 0.8 fusion.47
  73.9 1.5 fusion.68
  75.4 2.3 fusion.17
  77.7 0.8 copy.101
  78.6 1.3 copy-done.10
  79.9 4.6 %convolution_convert_fusion = bf16[512,4096]{1,0:T(8,128)(2,1)} fusion(bf16[512,4096]{1,0:T(8,128)(2,1)S(1)} %copy-done.10, f32[512]{0:T(512)S(1)} %copy-done.11, f32[512,512]{0,1:T(8,128)S(1)} %bitcast.109, bf16[512,512]{0,1:T(8,128)(2,1)S(1)} %copy.102), kind=kOutput, calls=%fused_computation.6 | convolution fusion | flops 2151677952 | bytes 9963520 | tf_op jit(solution)/shard_map/dot_general | solution.py:121
  84.6 0.7 all-gather.9.cloned.1.call-update
  85.4 0.5 all-gather.11.cloned.1.call-update
  86.0 0.6 multiply_reduce_fusion.2
  86.7 0.6 dynamic-slice
  88.4 40.4 %all-reduce = f32[512]{0:T(512)S(1)} all-reduce(f32[512]{0:T(512)S(1)} %multiply_reduce_fusion), channel_id=5, replica_groups=mesh['ctx'=16,'exp'=16] {'exp'}, use_global_device_ids=true, to_apply=%region_6.7.clone | all-reduce | flops 512 | bytes 4096
  128.9 63.8 %reduce-scatter.2.cloned.1.call-done = bf16[32,4096]{1,0:T(8,128)(2,1)} async-done(((bf16[512,4096]{1,0:T(8,128)(2,1)}), bf16[32,4096]{1,0:T(8,128)(2,1)}) %reduce-scatter.2.cloned.1.call-update) | async-done | bytes 262160 | tf_op jit(solution)/shard_map/reduce_scatter | solution.py:122
  192.6 1.2 multiply_reduce_fusion.1
  193.9 0.5 convolution_convert_fusion.2
  194.4 19.8 %all_to_all.10 = bf16[16,8,4096]{2,1,0:T(8,128)(2,1)S(1)} all-to-all(bf16[16,8,4096]{2,1,0:T(8,128)(2,1)S(1)} %convolution_convert_fusion.2), channel_id=1, replica_groups=mesh['ctx'=16,'exp'=16] {'exp'}, dimensions={0} | all-to-all | bytes 2097152 | tf_op jit(solution)/shard_map/all_to_all | solution.py:153
  214.5 53.0 %all-gather.9.cloned.1.call-done = bf16[1,4096,1536]{2,1,0:T(8,128)(2,1)} async-done(((bf16[1,256,1536]{2,1,0:T(8,128)(2,1)}), bf16[1,4096,1536]{2,1,0:T(8,128)(2,1)}) %all-gather.9.cloned.1.call-update) | async-done | bytes 12582928 | tf_op jit(solution)/shard_map/all_gather | solution.py:156
  267.5 6.6 %convolution_convert_fusion.1 = bf16[16,128,1536]{2,1,0:T(8,128)(2,1)S(1)} fusion(bf16[16,256,1536]{2,1,0:T(8,128)(2,1)} %bitcast.107, bf16[128,16,256]{2,1,0:T(8,128)(2,1)S(1)} %bitcast.108), kind=kOutput, calls=%fused_computation.7 | convolution fusion | flops 1613758464 | bytes 19922944 | tf_op jit(solution)/shard_map/rkw,kwf->krf/dot_general | solution.py:158
  274.1 0.9 convert_reduce_fusion
  275.0 40.1 %all-gather.11.cloned.1.call-done = bf16[1,4096,768]{2,1,0:T(8,128)(2,1)} async-done(((bf16[1,256,768]{2,1,0:T(8,128)(2,1)}), bf16[1,4096,768]{2,1,0:T(8,128)(2,1)}) %all-gather.11.cloned.1.call-update) | async-done | bytes 6291472 | tf_op jit(solution)/shard_map/all_gather | solution.py:169
  315.1 5.9 %fusion.5 = bf16[16,8,4096]{2,1,0:T(8,128)(2,1)} fusion(bf16[1,4096,768]{2,1,0:T(8,128)(2,1)} %all-gather.11.cloned.1.call-done, f32[128,1536]{1,0:T(8,128)S(1)} %convert_reduce_fusion), kind=kOutput, calls=%fused_computation.10 | convolution fusion | flops 806420480 | bytes 8126464 | tf_op jit(solution)/shard_map/rf,df->rd/dot_general | solution.py:166
  321.0 6.8 %all-to-all-start.1 = ((bf16[16,8,4096]{2,1,0:T(8,128)(2,1)}), bf16[16,8,4096]{2,1,0:T(8,128)(2,1)S(1)}, u32[]{:S(2)}, u32[]{:S(2)}) async-start(bf16[16,8,4096]{2,1,0:T(8,128)(2,1)} %fusion.5), calls=%async_computation.2 | async-start | bytes 2097152 | tf_op jit(solution)/shard_map/all_to_all | solution.py:172
  328.4 17.6 %all-to-all-done.1 = bf16[16,8,4096]{2,1,0:T(8,128)(2,1)S(1)} async-done(((bf16[16,8,4096]{2,1,0:T(8,128)(2,1)}), bf16[16,8,4096]{2,1,0:T(8,128)(2,1)S(1)}, u32[]{:S(2)}, u32[]{:S(2)}) %all-to-all-start.1) | async-done | bytes 1048608 | tf_op jit(solution)/shard_map/all_to_all | solution.py:172
  346.0 1.5 convolution_bitcast_fusion
  (73 shorter events, 4.3 us)
Async XLA Ops:
  7.2 320.6 %copy-start = (bf16[4096,72]{0,1:T(8,128)(2,1)S(1)}, bf16[4096,72]{0,1:T(8,128)(2,1)}, u32[]{:S(2)}) copy-start(bf16[4096,72]{0,1:T(8,128)(2,1)} %param.31) | copy-start | bytes 1769476
  7.2 61.5 %all-gather.7.cloned.1.call-start = ((), (), s32[]{:S(2)}) async-start(), calls=%async_computation.3 | async-start | bytes 4456448 | tf_op jit(solution)/shard_map/all_gather | solution.py:26
  9.5 10.3 %collective-permute-start = (bf16[3,768]{0,1:T(8,128)(2,1)}, bf16[3,768]{0,1:T(8,128)(2,1)S(1)}, u32[]{:S(2)}, u32[]{:S(2)}) collective-permute-start(bf16[3,768]{0,1:T(8,128)(2,1)} %copy.91), channel_id=1, source_target_pairs={{0,16},{16,32},{32,48},{48,64},{64,80},{80,96},{96,112},{112,128},... | collective-permute-start | bytes 13832 | tf_op jit(solution)/shard_map/ppermute | solution.py:21
  17.5 5.2 %copy-start.8 = (f32[8]{0:T(128)}, f32[8]{0:T(128)S(1)}, u32[]{:S(2)}) copy-start(f32[8]{0:T(128)S(1)} %broadcast_multiply_fusion) | copy-start | bytes 100
  19.7 3.9 %copy-start.4 = (bf16[512,512]{1,0:T(8,128)(2,1)S(1)}, bf16[512,512]{1,0:T(8,128)(2,1)}, u32[]{:S(2)}) copy-start(bf16[512,512]{1,0:T(8,128)(2,1)} %param.20) | copy-start | bytes 1572868
  20.4 48.3 %copy-start.2 = (bf16[512,128]{1,0:T(8,128)(2,1)}, bf16[512,128]{1,0:T(8,128)(2,1)S(1)}, u32[]{:S(2)}) copy-start(bf16[512,128]{1,0:T(8,128)(2,1)S(1)} %get-tuple-element.87) | copy-start | bytes 393220
  23.5 169.1 %reduce-scatter.2.cloned.1.call-start = ((), (), s32[]{:S(2)}) async-start(), calls=%async_computation.4 | async-start | bytes 4456448 | tf_op jit(solution)/shard_map/reduce_scatter | solution.py:122
  72.8 2.5 copy-start.3
  77.7 2.2 copy-start.10
  77.7 2.2 copy-start.11
  84.5 1.4 copy-start.6
  84.5 1.4 copy-start.9
  84.5 2.2 copy-start.12
  84.5 108.1 %copy-start.5 = (bf16[32,4096]{1,0:T(8,128)(2,1)S(1)}, bf16[32,4096]{1,0:T(8,128)(2,1)}, u32[]{:S(2)}) copy-start(bf16[32,4096]{1,0:T(8,128)(2,1)} %param.29) | copy-start | bytes 786436
  84.6 109.3 %copy-start.7 = (f32[4096]{0:T(1024)S(1)}, f32[4096]{0:T(1024)}, u32[]{:S(2)}) copy-start(f32[4096]{0:T(1024)} %param.30) | copy-start | bytes 49156
  84.6 182.9 %all-gather.9.cloned.1.call-start = ((), (), s32[]{:S(2)}) async-start(), calls=%async_computation.5 | async-start | bytes 13369344 | tf_op jit(solution)/shard_map/all_gather | solution.py:156
  85.3 229.7 %all-gather.11.cloned.1.call-start = ((), (), s32[]{:S(2)}) async-start(), calls=%async_computation.6 | async-start | bytes 6684672 | tf_op jit(solution)/shard_map/all_gather | solution.py:169
  193.9 133.9 %copy-start.1 = (f32[32,4096]{1,0:T(8,128)}, f32[32,4096]{1,0:T(8,128)S(1)}, u32[]{:S(2)}) copy-start(f32[32,4096]{1,0:T(8,128)S(1)} %get-tuple-element.83) | copy-start | bytes 1572868
  321.0 25.0 %all-to-all-start.1 = ((bf16[16,8,4096]{2,1,0:T(8,128)(2,1)}), bf16[16,8,4096]{2,1,0:T(8,128)(2,1)S(1)}, u32[]{:S(2)}, u32[]{:S(2)}) async-start(bf16[16,8,4096]{2,1,0:T(8,128)(2,1)} %fusion.5), calls=%async_computation.2 | async-start | bytes 2097152 | tf_op jit(solution)/shard_map/all_to_all | solution.py:172
Sparse Core Ops, SparseCore 0:
  23.6 44.9 all-gather.6
  84.7 107.8 reduce-scatter.1
  194.5 72.9 all-gather.8
  269.2 45.8 all-gather.10
where the time goes:
time: 356 us; the launch traced here: 354 us
  waiting for transfers between devices  200 us (56%)
  blocking collectives  79.3 us (22%)
  matrix products  25.1 us (7%)
  between operations  14.8 us (4%)
  local copies, waits for them, and re-layouts  13.1 us (4%)
  other arithmetic  13.1 us (4%)
  starting transfers between devices  8.84 us (2%)
    reduce_scatter x1, waiting for transfers between devices, body(): lax.psum_scatter(projected.astype(jnp.bfloat16), 'exp', scatter_dimension...  63.8 us
    all_gather x1, waiting for transfers between devices, body(): whole_in = lax.all_gather(expert_in[0], 'ctx', axis=0, tiled=True)  53 us
    unnamed x1, blocking collectives  40.4 us
    all_gather x1, waiting for transfers between devices, body(): lax.all_gather(expert_out[0], 'ctx', axis=0, tiled=True)  40.1 us
    all_gather x1, waiting for transfers between devices, carried_in(): gathered = jax.tree.map(lambda a: lax.all_gather(a, axis), part)  24.1 us
    all_to_all x1, blocking collectives, body(): lax.all_to_all(outbound, 'exp', split_axis=0, concat_axis=0, tiled=True)  19.8 us
    all_gather x1, blocking collectives, carried_in(): gathered = jax.tree.map(lambda a: lax.all_gather(a, axis), part)  19 us
    all_to_all x1, waiting for transfers between devices, body(): lax.all_to_all(answer.reshape(flight, capacity, answer.shape[1]), 'exp',...  17.6 us
  transfers between devices with their start and end apart: 6, of which 5 were waited for; matrix products, arithmetic and copies ran while one was open for 6% of the time, Pallas kernels for 0%

commit v1 on v0

--- a/solution.py
+++ b/solution.py
@@ -2,6 +2,7 @@
 import jax.numpy as jnp
 from jax import lax
 from jax.sharding import PartitionSpec as P
+from jax.lax import axis_index, ppermute, psum
 
 HDIM = 64
 STATE = 128
@@ -13,6 +14,40 @@
 INNER = 8192
 EPS = 1e-05
 HIGH = lax.Precision.HIGHEST
+
+
+def waves_trace(buf, dim_no):
+    buf = jnp.moveaxis(buf, 0, dim_no)
+    lower = buf.shape
+    long_array = buf.reshape(
+        *lower[:dim_no], lower[dim_no] * lower[dim_no + 1], *lower[dim_no + 2 :]
+    )
+    return long_array
+
+
+def _try_all_forms(x_part, named_axis, k_dim):
+    total_devices = psum(1, axis_name=named_axis)
+    pool = tuple(((u, (u + 1) % total_devices) for u in range(total_devices)))
+    part_next, current_block = ([], [])
+    xs_all = tuple(((w, idx) for idx, w in pool))
+    for p in range(total_devices - 1):
+        if p % 2 == 0:
+            part_next.append(
+                ppermute(part_next[-1] if part_next else x_part, axis_name=named_axis, perm=pool)
+            )
+        else:
+            current_block.append(
+                ppermute(
+                    current_block[-1] if current_block else x_part,
+                    axis_name=named_axis,
+                    perm=xs_all,
+                )
+            )
+    back = jnp.stack([*part_next[::-1], x_part, *current_block])
+    all_rows = axis_index(named_axis) - len(part_next)
+    back = back[(jnp.arange(total_devices) - all_rows) % total_devices]
+    o_now = waves_trace(back, k_dim)
+    return o_now
 
 
 def shifted(array, axis, by):
@@ -166,7 +201,7 @@
     answer = jnp.einsum(
         "rf,df->rd",
         activated,
-        lax.all_gather(expert_out[0], "ctx", axis=0, tiled=True),
+        _try_all_forms(expert_out[0], "ctx", 0),
         preferred_element_type=jnp.float32,
     ).astype(jnp.bfloat16)
     returned = lax.all_to_all(

time: 356 us -> 305 us (0.86)
  waiting for transfers between devices: 200 us -> 99.3 us
  starting transfers between devices: 8.84 us -> 45 us
  local copies, waits for them, and re-layouts: 13.1 us -> 45.1 us
  blocking collectives: 79.3 us -> 58.8 us
    reduce_scatter x1, waiting for transfers between devices: 63.8 us -> 0.01 us  [body(): lax.psum_scatter(projected.astype(jnp.bfloat16), 'exp', scatter_dimension...]
    ppermute x0 -> x15, waiting for transfers between devices: none -> 41.3 us  [the longest x8 39.5 us: _try_all_forms(): ppermute(part_next[-1] if part_next else x_part, axis_name=named_axis, pe...]
    all_gather x1 -> x0, waiting for transfers between devices: 40.1 us -> none  [body(): lax.all_gather(expert_out[0], 'ctx', axis=0, tiled=True)]
    all_gather x1, waiting for transfers between devices: 53 us -> 16.7 us  [body(): whole_in = lax.all_gather(expert_in[0], 'ctx', axis=0, tiled=True)]
    ppermute x0 -> x15, starting transfers between devices: none -> 31.8 us  [the longest x7 28.5 us: _try_all_forms(): ppermute(current_block[-1] if current_block else x_part, axis_name=named_...]
    unnamed x31 -> x68, local copies, waits for them, and re-layouts: 3.72 us -> 28.3 us
    all_to_all x1 -> x0, blocking collectives: 19.8 us -> none  [body(): lax.all_to_all(outbound, 'exp', split_axis=0, concat_axis=0, tiled=True)]
    gather x0 -> x1, local copies, waits for them, and re-layouts: none -> 6.46 us  [_try_all_forms(): back = back[(jnp.arange(total_devices) - all_rows) % total_devices]]
  transfers between devices with their start and end apart: 6 -> 21, of which waited for: 5 -> 12; matrix products, arithmetic and copies ran while one was open for 6% -> 17% of each run, Pallas kernels for 0% -> 0%
where the time goes in v1:
time: 305 us; the launch traced here: 302 us
  waiting for transfers between devices  99.3 us (33%)
  blocking collectives  58.8 us (19%)
  local copies, waits for them, and re-layouts  45.1 us (15%)
  starting transfers between devices  45 us (15%)
  matrix products  25 us (8%)
  between operations  14.9 us (5%)
  other arithmetic  13.8 us (5%)
    unnamed x1, blocking collectives  40.7 us
    ppermute x8, waiting for transfers between devices, _try_all_forms(): ppermute(part_next[-1] if part_next else x_part, axis_name=named_axis, pe...  39.5 us
    ppermute x7, starting transfers between devices, _try_all_forms(): ppermute(current_block[-1] if current_block else x_part, axis_name=named_...  28.5 us
    unnamed x68, local copies, waits for them, and re-layouts  28.3 us
    all_gather x1, waiting for transfers between devices, carried_in(): gathered = jax.tree.map(lambda a: lax.all_gather(a, axis), part)  23 us
    all_gather x1, blocking collectives, carried_in(): gathered = jax.tree.map(lambda a: lax.all_gather(a, axis), part)  18.1 us
    all_to_all x1, waiting for transfers between devices, body(): lax.all_to_all(answer.reshape(flight, capacity, answer.shape[1]), 'exp',...  17.6 us
    all_gather x1, waiting for transfers between devices, body(): whole_in = lax.all_gather(expert_in[0], 'ctx', axis=0, tiled=True)  16.7 us
  transfers between devices with their start and end apart: 21, of which 12 were waited for; matrix products, arithmetic and copies ran while one was open for 17% of the time, Pallas kernels for 0%

profile of v1, /device:TPU:32, one launch (start us, length us, event | category | flops | bytes accessed | tf_op | source)
XLA Modules:
  0.0 302.0 jit_solution(6567205525784470750)
XLA Ops:
  8.9 1.9 collective-permute-start
  14.8 1.4 fusion.60
  20.8 2.2 multiply_convert_fusion.9
  26.7 18.1 %all-gather.1 = f32[16,1,8]{2,1,0:T(1,128)S(1)} all-gather(f32[1,1,8]{2,1,0:T(1,128)} %get-tuple-element.98), channel_id=1, replica_groups=mesh['ctx'=16,'exp'=16] {'ctx'}, dimensions={0}, use_global_device_ids=true | all-gather | bytes 544 | tf_op jit(solution)/shard_map/all_gather | solution.py:61
  45.5 2.0 fusion.62
  47.5 23.0 %all-gather.5.cloned.1.call-done = f32[16,8,128,64]{2,3,1,0:T(8,128)} async-done(((f32[1,8,128,64]{2,3,1,0:T(8,128)}), f32[16,8,128,64]{2,3,1,0:T(8,128)}) %all-gather.5.cloned.1.call-update) | async-done | bytes 4194320 | tf_op jit(solution)/shard_map/all_gather | solution.py:61
  70.6 2.8 while.12
  73.7 1.5 fusion.63
  75.2 2.7 fusion.10
  78.9 4.5 %convolution_convert_fusion = bf16[512,4096]{1,0:T(8,128)(2,1)} fusion(bf16[512,4096]{1,0:T(8,128)(2,1)S(1)} %copy-done.18, f32[512]{0:T(512)S(1)} %copy-done.19, f32[512,512]{0,1:T(8,128)S(1)} %bitcast.140, bf16[512,512]{0,1:T(8,128)(2,1)S(1)} %copy.102), kind=kOutput, calls=%fused_computation.5 | convolution fusion | flops 2151677952 | bytes 9963520 | tf_op jit(solution)/shard_map/dot_general | solution.py:156
  84.2 1.6 collective-permute-start.1
  85.9 5.6 %collective-permute-done.1 = bf16[256,768]{1,0:T(8,128)(2,1)S(1)} collective-permute-done((bf16[256,768]{1,0:T(8,128)(2,1)S(1)}, bf16[256,768]{1,0:T(8,128)(2,1)S(1)}, u32[]{:S(2)}, u32[]{:S(2)}) %collective-permute-start.1) | collective-permute-done | bytes 393248 | tf_op jit(solution)/shard_map/ppermute | solution.py:36
  93.2 5.5 %collective-permute-done.2 = bf16[256,768]{1,0:T(8,128)(2,1)S(1)} collective-permute-done((bf16[256,768]{1,0:T(8,128)(2,1)S(1)}, bf16[256,768]{1,0:T(8,128)(2,1)S(1)}, u32[]{:S(2)}, u32[]{:S(2)}) %collective-permute-start.2) | collective-permute-done | bytes 393248 | tf_op jit(solution)/shard_map/ppermute | solution.py:36
  99.5 12.2 %collective-permute-start.10 = (bf16[256,768]{1,0:T(8,128)(2,1)S(1)}, bf16[256,768]{1,0:T(8,128)(2,1)S(1)}, u32[]{:S(2)}, u32[]{:S(2)}) collective-permute-start(bf16[256,768]{1,0:T(8,128)(2,1)S(1)} %collective-permute-done.9), channel_id=1, source_target_pairs={{16,0},{32,16},{48,32},{64,48},{80,64},{96,80},{112,96},{128,112},... | collective-permute-start | bytes 1179656 | tf_op jit(solution)/shard_map/ppermute | solution.py:40
  111.7 5.3 %collective-permute-done.3 = bf16[256,768]{1,0:T(8,128)(2,1)S(1)} collective-permute-done((bf16[256,768]{1,0:T(8,128)(2,1)S(1)}, bf16[256,768]{1,0:T(8,128)(2,1)S(1)}, u32[]{:S(2)}, u32[]{:S(2)}) %collective-permute-start.3) | collective-permute-done | bytes 393248 | tf_op jit(solution)/shard_map/ppermute | solution.py:36
  117.1 3.1 %collective-permute-start.11 = (bf16[256,768]{1,0:T(8,128)(2,1)S(1)}, bf16[256,768]{1,0:T(8,128)(2,1)S(1)}, u32[]{:S(2)}, u32[]{:S(2)}) collective-permute-start(bf16[256,768]{1,0:T(8,128)(2,1)S(1)} %collective-permute-done.10), channel_id=1, source_target_pairs={{16,0},{32,16},{48,32},{64,48},{80,64},{96,80},{112,96},{128,112},... | collective-permute-start | bytes 1179656 | tf_op jit(solution)/shard_map/ppermute | solution.py:40
  120.2 5.3 %collective-permute-done.4 = bf16[256,768]{1,0:T(8,128)(2,1)S(1)} collective-permute-done((bf16[256,768]{1,0:T(8,128)(2,1)S(1)}, bf16[256,768]{1,0:T(8,128)(2,1)S(1)}, u32[]{:S(2)}, u32[]{:S(2)}) %collective-permute-start.4) | collective-permute-done | bytes 393248 | tf_op jit(solution)/shard_map/ppermute | solution.py:36
  125.5 3.1 %collective-permute-start.12 = (bf16[256,768]{1,0:T(8,128)(2,1)S(1)}, bf16[256,768]{1,0:T(8,128)(2,1)}, u32[]{:S(2)}, u32[]{:S(2)}) collective-permute-start(bf16[256,768]{1,0:T(8,128)(2,1)S(1)} %collective-permute-done.11), channel_id=1, source_target_pairs={{16,0},{32,16},{48,32},{64,48},{80,64},{96,80},{112,96},{128,112},... | collective-permute-start | bytes 1179656 | tf_op jit(solution)/shard_map/ppermute | solution.py:40
  128.6 5.3 %collective-permute-done.5 = bf16[256,768]{1,0:T(8,128)(2,1)S(1)} collective-permute-done((bf16[256,768]{1,0:T(8,128)(2,1)S(1)}, bf16[256,768]{1,0:T(8,128)(2,1)S(1)}, u32[]{:S(2)}, u32[]{:S(2)}) %collective-permute-start.5) | collective-permute-done | bytes 393248 | tf_op jit(solution)/shard_map/ppermute | solution.py:36
  134.6 3.0 collective-permute-start.13
  137.6 4.8 %collective-permute-done.6 = bf16[256,768]{1,0:T(8,128)(2,1)} collective-permute-done((bf16[256,768]{1,0:T(8,128)(2,1)S(1)}, bf16[256,768]{1,0:T(8,128)(2,1)}, u32[]{:S(2)}, u32[]{:S(2)}) %collective-permute-start.6) | collective-permute-done | bytes 393248 | tf_op jit(solution)/shard_map/ppermute | solution.py:36
  144.4 3.0 collective-permute-start.14
  147.4 3.8 %collective-permute-done.7 = bf16[256,768]{1,0:T(8,128)(2,1)} collective-permute-done((bf16[256,768]{1,0:T(8,128)(2,1)}, bf16[256,768]{1,0:T(8,128)(2,1)}, u32[]{:S(2)}, u32[]{:S(2)}) %collective-permute-start.7) | collective-permute-done | bytes 393248 | tf_op jit(solution)/shard_map/ppermute | solution.py:36
  151.2 1.8 collective-permute-done.14
  153.0 3.3 %collective-permute-start.15 = (bf16[256,768]{1,0:T(8,128)(2,1)}, bf16[256,768]{1,0:T(8,128)(2,1)}, u32[]{:S(2)}, u32[]{:S(2)}) collective-permute-start(bf16[256,768]{1,0:T(8,128)(2,1)} %collective-permute-done.14), channel_id=1, source_target_pairs={{16,0},{32,16},{48,32},{64,48},{80,64},{96,80},{112,96},{128,112},... | collective-permute-start | bytes 1179656 | tf_op jit(solution)/shard_map/ppermute | solution.py:40
  156.3 4.0 %collective-permute-done.8 = bf16[256,768]{1,0:T(8,128)(2,1)S(1)} collective-permute-done((bf16[256,768]{1,0:T(8,128)(2,1)}, bf16[256,768]{1,0:T(8,128)(2,1)S(1)}, u32[]{:S(2)}, u32[]{:S(2)}) %collective-permute-start.8) | collective-permute-done | bytes 393248 | tf_op jit(solution)/shard_map/ppermute | solution.py:36
  161.0 1.8 bitcast_dynamic-update-slice_fusion.13
  162.8 1.8 bitcast_dynamic-update-slice_fusion.12
  164.6 1.8 bitcast_dynamic-update-slice_fusion.11
  166.3 1.8 bitcast_dynamic-update-slice_fusion.10
  168.1 1.8 bitcast_dynamic-update-slice_fusion.9
  169.9 1.8 bitcast_dynamic-update-slice_fusion.8
  175.2 40.7 %all-reduce = f32[512]{0:T(512)S(1)} all-reduce(f32[512]{0:T(512)S(1)} %multiply_reduce_fusion), channel_id=4, replica_groups=mesh['ctx'=16,'exp'=16] {'exp'}, use_global_device_ids=true, to_apply=%region_6.7.clone | all-reduce | flops 512 | bytes 4096
  217.3 1.5 convolution_convert_fusion.3
  218.8 4.3 %all-to-all-start = ((bf16[16,8,4096]{2,1,0:T(8,128)(2,1)}), bf16[16,8,4096]{2,1,0:T(8,128)(2,1)}, u32[]{:S(2)}, u32[]{:S(2)}) async-start(bf16[16,8,4096]{2,1,0:T(8,128)(2,1)} %convolution_convert_fusion.3), calls=%async_computation.1 | async-start | bytes 2097152 | tf_op jit(solution)/shard_map/all_to_all | solution.py:188
  223.1 1.8 bitcast_dynamic-update-slice_fusion.4
  224.9 1.8 bitcast_dynamic-update-slice_fusion.3
  226.7 1.8 bitcast_dynamic-update-slice_fusion.2
  228.5 1.8 bitcast_dynamic-update-slice_fusion.1
  230.3 1.8 bitcast_dynamic-update-slice_fusion
  232.1 6.5 %gather_fusion = bf16[16,256,768]{2,1,0:T(8,128)(2,1)} fusion(bf16[16,256,768]{2,1,0:T(8,128)(2,1)} %bitcast_dynamic-update-slice_fusion, s32[1024]{0:T(1024)S(1)} %pad_clamp_fusion), kind=kCustom, calls=%fused_computation | custom fusion | bytes 12582976 | tf_op jit(solution)/shard_map/gather | solution.py:48
  238.5 2.6 copy.111
  241.2 16.7 %all-gather.7.cloned.1.call-done = bf16[1,4096,1536]{2,1,0:T(8,128)(2,1)} async-done(((bf16[1,256,1536]{2,1,0:T(8,128)(2,1)}), bf16[1,4096,1536]{2,1,0:T(8,128)(2,1)}) %all-gather.7.cloned.1.call-update) | async-done | bytes 12582928 | tf_op jit(solution)/shard_map/all_gather | solution.py:191
  257.8 7.1 %convolution_convert_fusion.1 = bf16[16,128,1536]{2,1,0:T(8,128)(2,1)S(1)} fusion(bf16[16,256,1536]{2,1,0:T(8,128)(2,1)} %bitcast.135, bf16[128,16,256]{2,1,0:T(8,128)(2,1)} %bitcast.139), kind=kOutput, calls=%fused_computation.6 | convolution fusion | flops 1613758464 | bytes 19922944 | tf_op jit(solution)/shard_map/rkw,kwf->krf/dot_general | solution.py:193
  265.8 3.1 %fusion = bf16[16,8,4096]{2,1,0:T(8,128)(2,1)} fusion(bf16[4096,768]{1,0:T(8,128)(2,1)S(1)} %bitcast.138, f32[128,1536]{1,0:T(8,128)S(1)} %convert_reduce_fusion), kind=kOutput, calls=%fused_computation.9 | convolution fusion | flops 806420480 | bytes 8126464 | tf_op jit(solution)/shard_map/rf,df->rd/dot_general | solution.py:201
  268.9 6.8 %all-to-all-start.1 = ((bf16[16,8,4096]{2,1,0:T(8,128)(2,1)}), bf16[16,8,4096]{2,1,0:T(8,128)(2,1)S(1)}, u32[]{:S(2)}, u32[]{:S(2)}) async-start(bf16[16,8,4096]{2,1,0:T(8,128)(2,1)} %fusion), calls=%async_computation.2 | async-start | bytes 2097152 | tf_op jit(solution)/shard_map/all_to_all | solution.py:207
  276.4 17.6 %all-to-all-done.1 = bf16[16,8,4096]{2,1,0:T(8,128)(2,1)S(1)} async-done(((bf16[16,8,4096]{2,1,0:T(8,128)(2,1)}), bf16[16,8,4096]{2,1,0:T(8,128)(2,1)S(1)}, u32[]{:S(2)}, u32[]{:S(2)}) %all-to-all-start.1) | async-done | bytes 1048608 | tf_op jit(solution)/shard_map/all_to_all | solution.py:207
  294.0 1.5 convolution_bitcast_fusion
  (143 shorter events, 31.1 us)
Async XLA Ops:
  7.2 268.6 %copy-start = (bf16[4096,72]{0,1:T(8,128)(2,1)S(1)}, bf16[4096,72]{0,1:T(8,128)(2,1)}, u32[]{:S(2)}) copy-start(bf16[4096,72]{0,1:T(8,128)(2,1)} %param.31) | copy-start | bytes 1769476
  7.2 63.3 %all-gather.5.cloned.1.call-start = ((), (), s32[]{:S(2)}) async-start(), calls=%async_computation.3 | async-start | bytes 4456448 | tf_op jit(solution)/shard_map/all_gather | solution.py:61
  8.9 10.8 %collective-permute-start = (bf16[3,768]{0,1:T(8,128)(2,1)S(1)}, bf16[3,768]{0,1:T(8,128)(2,1)S(1)}, u32[]{:S(2)}, u32[]{:S(2)}) collective-permute-start(bf16[3,768]{0,1:T(8,128)(2,1)S(1)} %copy.91), channel_id=1, source_target_pairs={{0,16},{16,32},{32,48},{48,64},{64,80},{80,96},{96,112},{112,128},... | collective-permute-start | bytes 13832 | tf_op jit(solution)/shard_map/ppermute | solution.py:56
  20.8 4.6 %copy-start.2 = (bf16[512,128]{1,0:T(8,128)(2,1)}, bf16[512,128]{1,0:T(8,128)(2,1)S(1)}, u32[]{:S(2)}) copy-start(bf16[512,128]{1,0:T(8,128)(2,1)S(1)} %get-tuple-element.86) | copy-start | bytes 393220
  25.3 190.6 %reduce-scatter.2.cloned.1.call-start = ((), (), s32[]{:S(2)}) async-start(), calls=%async_computation.4 | async-start | bytes 4456448 | tf_op jit(solution)/shard_map/reduce_scatter | solution.py:157
  70.5 3.0 copy-start.15
  70.5 3.0 copy-start.16
  70.5 4.6 %copy-start.20 = (f32[8]{0:T(128)S(1)}, f32[8]{0:T(128)}, u32[]{:S(2)}) copy-start(f32[8]{0:T(128)} %param.26) | copy-start | bytes 100
  75.2 3.7 %copy-start.18 = (bf16[512,4096]{1,0:T(8,128)(2,1)S(1)}, bf16[512,4096]{1,0:T(8,128)(2,1)}, u32[]{:S(2)}) copy-start(bf16[512,4096]{1,0:T(8,128)(2,1)} %param.28) | copy-start | bytes 12582916
  75.2 3.7 %copy-start.19 = (f32[512]{0:T(512)S(1)}, f32[512]{0:T(512)}, u32[]{:S(2)}) copy-start(f32[512]{0:T(512)} %param.27) | copy-start | bytes 6148
  78.9 5.4 %copy-start.3 = (bf16[1,256,768]{2,1,0:T(8,128)(2,1)S(1)}, bf16[1,256,768]{2,1,0:T(8,128)(2,1)}, u32[]{:S(2)}) copy-start(bf16[1,256,768]{2,1,0:T(8,128)(2,1)} %param.35) | copy-start | bytes 1179652
  78.9 55.0 %copy-start.17 = (s32[1,32]{1,0:T(1,128)S(1)}, s32[1,32]{1,0:T(1,128)}, u32[]{:S(2)}) copy-start(s32[1,32]{1,0:T(1,128)} %param.33) | copy-start | bytes 388
  78.9 63.5 %copy-start.13 = (s32[32,10]{0,1:T(8,128)S(1)}, s32[32,10]{0,1:T(8,128)}, u32[]{:S(2)}) copy-start(s32[32,10]{0,1:T(8,128)} %param.32) | copy-start | bytes 3844
  78.9 64.2 %copy-start.21 = (u32[256]{0:T(256)S(1)}, u32[256]{0:T(256)}, u32[]{:S(2)}) copy-start(u32[256]{0:T(256)} %constant.81) | copy-start | bytes 3076
  83.5 133.8 %copy-start.14 = (f32[4096]{0:T(1024)S(1)}, f32[4096]{0:T(1024)}, u32[]{:S(2)}) copy-start(f32[4096]{0:T(1024)} %param.30) | copy-start | bytes 49156
  83.5 174.3 %all-gather.7.cloned.1.call-start = ((), (), s32[]{:S(2)}) async-start(), calls=%async_computation.5 | async-start | bytes 13369344 | tf_op jit(solution)/shard_map/all_gather | solution.py:191
  84.2 7.2 %collective-permute-start.1 = (bf16[256,768]{1,0:T(8,128)(2,1)S(1)}, bf16[256,768]{1,0:T(8,128)(2,1)S(1)}, u32[]{:S(2)}, u32[]{:S(2)}) collective-permute-start(bf16[256,768]{1,0:T(8,128)(2,1)S(1)} %bitcast.150), channel_id=1, source_target_pairs={{0,16},{16,32},{32,48},{48,64},{64,80},{80,96},{96,112},{112,128},... | collective-permute-start | bytes 1179656 | tf_op jit(solution)/shard_map/ppermute | solution.py:36
  91.5 7.2 %collective-permute-start.2 = (bf16[256,768]{1,0:T(8,128)(2,1)S(1)}, bf16[256,768]{1,0:T(8,128)(2,1)S(1)}, u32[]{:S(2)}, u32[]{:S(2)}) collective-permute-start(bf16[256,768]{1,0:T(8,128)(2,1)S(1)} %collective-permute-done.1), channel_id=1, source_target_pairs={{0,16},{16,32},{32,48},{48,64},{64,80},{80,96},{96,112},{112,128},... | collective-permute-start | bytes 1179656 | tf_op jit(solution)/shard_map/ppermute | solution.py:36
  92.3 7.2 %collective-permute-start.9 = (bf16[256,768]{1,0:T(8,128)(2,1)S(1)}, bf16[256,768]{1,0:T(8,128)(2,1)S(1)}, u32[]{:S(2)}, u32[]{:S(2)}) collective-permute-start(bf16[256,768]{1,0:T(8,128)(2,1)S(1)} %bitcast.151), channel_id=1, source_target_pairs={{16,0},{32,16},{48,32},{64,48},{80,64},{96,80},{112,96},{128,112},... | collective-permute-start | bytes 1179656 | tf_op jit(solution)/shard_map/ppermute | solution.py:40
  98.7 26.8 %copy-start.7 = (bf16[256,768]{1,0:T(8,128)(2,1)}, bf16[256,768]{1,0:T(8,128)(2,1)S(1)}, u32[]{:S(2)}) copy-start(bf16[256,768]{1,0:T(8,128)(2,1)S(1)} %collective-permute-done.2) | copy-start | bytes 1179652
  98.7 18.4 %collective-permute-start.3 = (bf16[256,768]{1,0:T(8,128)(2,1)S(1)}, bf16[256,768]{1,0:T(8,128)(2,1)S(1)}, u32[]{:S(2)}, u32[]{:S(2)}) collective-permute-start(bf16[256,768]{1,0:T(8,128)(2,1)S(1)} %collective-permute-done.2), channel_id=1, source_target_pairs={{0,16},{16,32},{32,48},{48,64},{64,80},{80,96},{96,112},{112,128},... | collective-permute-start | bytes 1179656 | tf_op jit(solution)/shard_map/ppermute | solution.py:36
  99.5 17.5 %copy-start.5 = (bf16[256,768]{1,0:T(8,128)(2,1)}, bf16[256,768]{1,0:T(8,128)(2,1)S(1)}, u32[]{:S(2)}) copy-start(bf16[256,768]{1,0:T(8,128)(2,1)S(1)} %collective-permute-done.9) | copy-start | bytes 1179652
  99.5 17.5 %collective-permute-start.10 = (bf16[256,768]{1,0:T(8,128)(2,1)S(1)}, bf16[256,768]{1,0:T(8,128)(2,1)S(1)}, u32[]{:S(2)}, u32[]{:S(2)}) collective-permute-start(bf16[256,768]{1,0:T(8,128)(2,1)S(1)} %collective-permute-done.9), channel_id=1, source_target_pairs={{16,0},{32,16},{48,32},{64,48},{80,64},{96,80},{112,96},{128,112},... | collective-permute-start | bytes 1179656 | tf_op jit(solution)/shard_map/ppermute | solution.py:40
  117.0 16.8 %copy-start.10 = (bf16[256,768]{1,0:T(8,128)(2,1)}, bf16[256,768]{1,0:T(8,128)(2,1)S(1)}, u32[]{:S(2)}) copy-start(bf16[256,768]{1,0:T(8,128)(2,1)S(1)} %collective-permute-done.3) | copy-start | bytes 1179652
  117.0 8.4 %collective-permute-start.4 = (bf16[256,768]{1,0:T(8,128)(2,1)S(1)}, bf16[256,768]{1,0:T(8,128)(2,1)S(1)}, u32[]{:S(2)}, u32[]{:S(2)}) collective-permute-start(bf16[256,768]{1,0:T(8,128)(2,1)S(1)} %collective-permute-done.3), channel_id=1, source_target_pairs={{0,16},{16,32},{32,48},{48,64},{64,80},{80,96},{96,112},{112,128},... | collective-permute-start | bytes 1179656 | tf_op jit(solution)/shard_map/ppermute | solution.py:36
  117.1 11.5 %copy-start.8 = (bf16[256,768]{1,0:T(8,128)(2,1)}, bf16[256,768]{1,0:T(8,128)(2,1)S(1)}, u32[]{:S(2)}) copy-start(bf16[256,768]{1,0:T(8,128)(2,1)S(1)} %collective-permute-done.10) | copy-start | bytes 1179652
  117.1 8.4 %collective-permute-start.11 = (bf16[256,768]{1,0:T(8,128)(2,1)S(1)}, bf16[256,768]{1,0:T(8,128)(2,1)S(1)}, u32[]{:S(2)}, u32[]{:S(2)}) collective-permute-start(bf16[256,768]{1,0:T(8,128)(2,1)S(1)} %collective-permute-done.10), channel_id=1, source_target_pairs={{16,0},{32,16},{48,32},{64,48},{80,64},{96,80},{112,96},{128,112},... | collective-permute-start | bytes 1179656 | tf_op jit(solution)/shard_map/ppermute | solution.py:40
  125.4 8.4 %copy-start.11 = (bf16[256,768]{1,0:T(8,128)(2,1)}, bf16[256,768]{1,0:T(8,128)(2,1)S(1)}, u32[]{:S(2)}) copy-start(bf16[256,768]{1,0:T(8,128)(2,1)S(1)} %collective-permute-done.4) | copy-start | bytes 1179652
  125.4 8.4 %collective-permute-start.5 = (bf16[256,768]{1,0:T(8,128)(2,1)S(1)}, bf16[256,768]{1,0:T(8,128)(2,1)S(1)}, u32[]{:S(2)}, u32[]{:S(2)}) collective-permute-start(bf16[256,768]{1,0:T(8,128)(2,1)S(1)} %collective-permute-done.4), channel_id=1, source_target_pairs={{0,16},{16,32},{32,48},{48,64},{64,80},{80,96},{96,112},{112,128},... | collective-permute-start | bytes 1179656 | tf_op jit(solution)/shard_map/ppermute | solution.py:36
  125.5 90.5 %copy-start.4 = (bf16[256,768]{1,0:T(8,128)(2,1)}, bf16[256,768]{1,0:T(8,128)(2,1)S(1)}, u32[]{:S(2)}) copy-start(bf16[256,768]{1,0:T(8,128)(2,1)S(1)} %collective-permute-done.11) | copy-start | bytes 1179652
  125.5 8.5 %collective-permute-start.12 = (bf16[256,768]{1,0:T(8,128)(2,1)S(1)}, bf16[256,768]{1,0:T(8,128)(2,1)}, u32[]{:S(2)}, u32[]{:S(2)}) collective-permute-start(bf16[256,768]{1,0:T(8,128)(2,1)S(1)} %collective-permute-done.11), channel_id=1, source_target_pairs={{16,0},{32,16},{48,32},{64,48},{80,64},{96,80},{112,96},{128,112},... | collective-permute-start | bytes 1179656 | tf_op jit(solution)/shard_map/ppermute | solution.py:40
  133.9 0.7 copy-start.12
  133.9 8.5 %collective-permute-start.6 = (bf16[256,768]{1,0:T(8,128)(2,1)S(1)}, bf16[256,768]{1,0:T(8,128)(2,1)}, u32[]{:S(2)}, u32[]{:S(2)}) collective-permute-start(bf16[256,768]{1,0:T(8,128)(2,1)S(1)} %collective-permute-done.5), channel_id=1, source_target_pairs={{0,16},{16,32},{32,48},{48,64},{64,80},{80,96},{96,112},{112,128},... | collective-permute-start | bytes 1179656 | tf_op jit(solution)/shard_map/ppermute | solution.py:36
  134.6 9.8 %collective-permute-start.13 = (bf16[256,768]{1,0:T(8,128)(2,1)}, bf16[256,768]{1,0:T(8,128)(2,1)}, u32[]{:S(2)}, u32[]{:S(2)}) collective-permute-start(bf16[256,768]{1,0:T(8,128)(2,1)} %collective-permute-done.12), channel_id=1, source_target_pairs={{16,0},{32,16},{48,32},{64,48},{80,64},{96,80},{112,96},{128,112},... | collective-permute-start | bytes 1179656 | tf_op jit(solution)/shard_map/ppermute | solution.py:40
  142.4 8.8 %collective-permute-start.7 = (bf16[256,768]{1,0:T(8,128)(2,1)}, bf16[256,768]{1,0:T(8,128)(2,1)}, u32[]{:S(2)}, u32[]{:S(2)}) collective-permute-start(bf16[256,768]{1,0:T(8,128)(2,1)} %collective-permute-done.6), channel_id=1, source_target_pairs={{0,16},{16,32},{32,48},{48,64},{64,80},{80,96},{96,112},{112,128},... | collective-permute-start | bytes 1179656 | tf_op jit(solution)/shard_map/ppermute | solution.py:36
  144.4 28.9 %copy-start.6 = (bf16[256,768]{1,0:T(8,128)(2,1)S(1)}, bf16[256,768]{1,0:T(8,128)(2,1)}, u32[]{:S(2)}) copy-start(bf16[256,768]{1,0:T(8,128)(2,1)} %copy-done.5) | copy-start | bytes 1179652
  144.4 29.7 %copy-start.9 = (bf16[256,768]{1,0:T(8,128)(2,1)S(1)}, bf16[256,768]{1,0:T(8,128)(2,1)}, u32[]{:S(2)}) copy-start(bf16[256,768]{1,0:T(8,128)(2,1)} %copy-done.8) | copy-start | bytes 1179652
  144.4 8.6 %collective-permute-start.14 = (bf16[256,768]{1,0:T(8,128)(2,1)}, bf16[256,768]{1,0:T(8,128)(2,1)}, u32[]{:S(2)}, u32[]{:S(2)}) collective-permute-start(bf16[256,768]{1,0:T(8,128)(2,1)} %collective-permute-done.13), channel_id=1, source_target_pairs={{16,0},{32,16},{48,32},{64,48},{80,64},{96,80},{112,96},{128,112},... | collective-permute-start | bytes 1179656 | tf_op jit(solution)/shard_map/ppermute | solution.py:40
  151.1 9.1 %collective-permute-start.8 = (bf16[256,768]{1,0:T(8,128)(2,1)}, bf16[256,768]{1,0:T(8,128)(2,1)S(1)}, u32[]{:S(2)}, u32[]{:S(2)}) collective-permute-start(bf16[256,768]{1,0:T(8,128)(2,1)} %collective-permute-done.7), channel_id=1, source_target_pairs={{0,16},{16,32},{32,48},{48,64},{64,80},{80,96},{96,112},{112,128},... | collective-permute-start | bytes 1179656 | tf_op jit(solution)/shard_map/ppermute | solution.py:36
  153.0 77.3 %collective-permute-start.15 = (bf16[256,768]{1,0:T(8,128)(2,1)}, bf16[256,768]{1,0:T(8,128)(2,1)}, u32[]{:S(2)}, u32[]{:S(2)}) collective-permute-start(bf16[256,768]{1,0:T(8,128)(2,1)} %collective-permute-done.14), channel_id=1, source_target_pairs={{16,0},{32,16},{48,32},{64,48},{80,64},{96,80},{112,96},{128,112},... | collective-permute-start | bytes 1179656 | tf_op jit(solution)/shard_map/ppermute | solution.py:40
  217.3 58.5 %copy-start.1 = (f32[32,4096]{1,0:T(8,128)}, f32[32,4096]{1,0:T(8,128)S(1)}, u32[]{:S(2)}) copy-start(f32[32,4096]{1,0:T(8,128)S(1)} %get-tuple-element.83) | copy-start | bytes 1572868
  218.8 19.7 %all-to-all-start = ((bf16[16,8,4096]{2,1,0:T(8,128)(2,1)}), bf16[16,8,4096]{2,1,0:T(8,128)(2,1)}, u32[]{:S(2)}, u32[]{:S(2)}) async-start(bf16[16,8,4096]{2,1,0:T(8,128)(2,1)} %convolution_convert_fusion.3), calls=%async_computation.1 | async-start | bytes 2097152 | tf_op jit(solution)/shard_map/all_to_all | solution.py:188
  238.5 27.2 %slice-start = ((s8[6291456]{0:T(1024)(128)(4,1)}), s8[2097152]{0:T(1024)(128)(4,1)S(1)}, s32[]{:S(2)}) async-start(s8[6291456]{0:T(1024)(128)(4,1)} %bitcast.136), calls=%async_computation.6 | async-start | bytes 4194304
  257.8 8.0 %slice-start.1 = ((s8[6291456]{0:T(1024)(128)(4,1)}), s8[4194304]{0:T(1024)(128)(4,1)S(1)}, s32[]{:S(2)}) async-start(s8[6291456]{0:T(1024)(128)(4,1)} %bitcast.136), calls=%async_computation.7 | async-start | bytes 8388608
  268.9 25.0 %all-to-all-start.1 = ((bf16[16,8,4096]{2,1,0:T(8,128)(2,1)}), bf16[16,8,4096]{2,1,0:T(8,128)(2,1)S(1)}, u32[]{:S(2)}, u32[]{:S(2)}) async-start(bf16[16,8,4096]{2,1,0:T(8,128)(2,1)} %fusion), calls=%async_computation.2 | async-start | bytes 2097152 | tf_op jit(solution)/shard_map/all_to_all | solution.py:207
Sparse Core Ops, SparseCore 0:
  25.5 44.9 all-gather.4
  83.6 99.2 reduce-scatter.1
  184.8 72.9 all-gather.6
